TPU v7x, 256 devices: a whole 4x4x8 slice. The times are simulated.
256 devices in a mesh: inst: 8 (over y_hi, x), space: 32 (over z, y_lo, core).
Axes of the slice: x: 4, y: 4 (y_hi: 2, y_lo: 2; y = y_hi * 2 + y_lo), z: 8, core: 2. Of those that a mesh axis runs over, the one named last changes fastest.
Arguments:
- psi_start: float32 [5, 8, 256, 1024], P(None, 'inst', 'space'), may hold values from -6 to 6
- density: float32 [8, 256, 1024], P('inst', 'space'), may hold values from 0.8 to 1.25
- velocity: float32 [3, 8, 256, 1024], P(None, 'inst', 'space'), may hold values from -0.6 to 0.6
- pressure: float32 [8, 256, 1024], P('inst', 'space'), may hold values from 0.5 to 1
- obs_pos: float32 [3, 512], P(None, 'space'), may hold values from -16 to 16, as said below
- obs_weight: float32 [2, 512], P(None, 'space'), may hold values from -0.6 to 0.6
- obs_harmonic: int32 [512], P('space'), may hold values from 1 to 3
- panel_pos: float32 [3, 65536], replicated, may hold values from -1 to 1
- panel_normal: float32 [3, 65536], P(None, 'space'), may hold values from -5 to 5
- panel_cell: int32 [65536], P('space'), may hold values from 0 to 8191
- plane_nbr: int32 [4, 1024], replicated, may hold values from 0 to 1023
Outputs:
- adjoint: float32 [5, 8, 256, 1024], P(None, 'inst', 'space')
Inputs may be any that keep to these rules, and one draw needn't show every extreme that they name: `obs_pos`: observers lie between 8 and 16 from the anchor, outside the panels' cube. panel_cell[q] is an index into the 8 x 1024 cells of the slot's owner, layer panel_cell[q] // 1024.
All inputs are finite; a program needn't handle non-finite values.
Results may differ from a plain program's by a relative error of at most 0.0001.
Values sent between devices are 32-bit elements; how exact they have to be, the bound alone decides.
A program may use at most 64 MiB of HBM per device.

v0:
```python
import math
import jax
import jax.numpy as jnp
from jax import lax
from jax.sharding import PartitionSpec as P

ITERS = 3
GAMMA = 1.4
KWAVE = 0.7
RADIUS = 10.0
TAU = 0.05
DISSIP = 0.25
OMEGA = 1.5
VISCO = 0.5


def padded_2(cells, sides, width):
    for axis, dim in sides:
        count = lax.axis_size(axis)
        head = lax.slice_in_dim(cells, 0, width, axis=dim)
        tail = lax.slice_in_dim(cells, cells.shape[dim] - width, cells.shape[dim], axis=dim)
        cells = jnp.concatenate(
            [
                lax.ppermute(tail, axis, [(i, (i + 1) % count) for i in range(count)]),
                cells,
                lax.ppermute(head, axis, [((i + 1) % count, i) for i in range(count)]),
            ],
            axis=dim,
        )
    return cells


def panel_block(observers, panels, time_now):
    delta = panels[:, None, :] - observers[:3, :, None]
    dist2 = jnp.sum(delta * delta, axis=0)
    dist = jnp.sqrt(dist2)
    harm = observers[5][:, None]
    phase = harm * (time_now - KWAVE * dist)
    amp = (
        (observers[3][:, None] * jnp.cos(phase) + observers[4][:, None] * jnp.sin(phase))
        * (RADIUS * RADIUS)
        / (dist2 * dist)
    )
    return jnp.sum(amp[None] * delta, axis=1)


def sensitivity(observers, panels, time_now):
    count = panels.shape[1]
    obs_count = observers.shape[1]
    block = math.gcd(count, max(128, 262144 // obs_count))
    split = panels.reshape(3, count // block, block).transpose(1, 0, 2)
    out = lax.map(lambda piece: panel_block(observers, piece, time_now), split)
    return out.transpose(1, 0, 2).reshape(3, count)


def conserved(density, velocity, pressure):
    moment = density[None] * velocity
    energy = pressure / (GAMMA - 1.0) + 0.5 * density * jnp.sum(velocity * velocity, axis=0)
    return jnp.concatenate([density[None], moment, energy[None]], axis=0)


def fluxes(state):
    dens = state[0]
    moment = state[1:4]
    energy = state[4]
    vel = moment / dens
    press = (GAMMA - 1.0) * (energy - 0.5 * jnp.sum(moment * vel, axis=0))
    result = []
    for axis_d in range(3):
        comps = [moment[axis_d]]
        for axis_e in range(3):
            term = moment[axis_e] * vel[axis_d]
            if axis_e == axis_d:
                term = term + press
            comps.append(term)
        comps.append((energy + press) * vel[axis_d])
        result.append(jnp.stack(comps))
    return tuple(result)


def spectral_coeff(offset, count):
    safe = jnp.where(offset == 0, 1.0, offset)
    angle = math.pi * safe / count
    even_odd_flag = 1.0 - 2.0 * jnp.mod(safe, 2.0)
    other = (
        -(OMEGA / 2.0) * even_odd_flag * jnp.cos(angle) / jnp.sin(angle)
        + VISCO * (OMEGA * OMEGA / 2.0) * even_odd_flag / jnp.sin(angle) ** 2
    )
    return jnp.where(offset == 0, VISCO * OMEGA * OMEGA * (count * count + 2.0) / 12.0, other)


def shards(
    psi_start,
    density,
    velocity,
    pressure,
    obs_pos,
    obs_weight,
    obs_harmonic,
    panel_pos,
    panel_normal,
    panel_cell,
    plane_nbr,
):
    inst_count = lax.axis_size("inst")
    inst_id = lax.axis_index("inst")
    space_id = lax.axis_index("space")
    time_now = 2.0 * math.pi * inst_id.astype(jnp.float32) / inst_count
    observers = jnp.concatenate(
        [obs_pos, obs_weight, obs_harmonic[None].astype(jnp.float32)], axis=0
    )
    owned_count = panel_normal.shape[1]
    whole = sensitivity(observers, panel_pos, time_now)
    total = lax.psum(whole, "space")
    sens = lax.dynamic_slice_in_dim(total, space_id * owned_count, owned_count, 1)
    weight = jnp.sum(sens * panel_normal, axis=0)
    layers = psi_start.shape[2]
    plane = psi_start.shape[3]
    wall = jax.ops.segment_sum(weight, panel_cell, num_segments=layers * plane).reshape(
        layers, plane
    )
    dens = density[0]
    vel = velocity[:, 0]
    state = conserved(dens, vel, pressure[0])
    slope = jnp.concatenate(
        [0.5 * jnp.sum(vel * vel, axis=0)[None], -vel, jnp.ones_like(dens)[None]], axis=0
    ) * (GAMMA - 1.0)
    source = slope * wall[None]
    _, pull = jax.vjp(fluxes, state)
    psi = psi_start[:, 0]
    for step in range(ITERS):
        padded = padded_2(psi, (("space", 1),), 1)
        minus_a = padded[:, :-2]
        plus_a = padded[:, 2:]
        plus_y = jnp.take(psi, plane_nbr[0], axis=2)
        minus_y = jnp.take(psi, plane_nbr[1], axis=2)
        plus_z = jnp.take(psi, plane_nbr[2], axis=2)
        minus_z = jnp.take(psi, plane_nbr[3], axis=2)
        middle_point = pull(
            (0.5 * (minus_a - plus_a), 0.5 * (minus_y - plus_y), 0.5 * (minus_z - plus_z))
        )[0]
        spread = 6.0 * psi - (minus_a + plus_a + plus_y + minus_y + plus_z + minus_z)
        every_instant = lax.all_gather(psi[:, None], "inst", axis=1, tiled=True)
        others = jnp.arange(inst_count, dtype=jnp.int32)
        row_entry = spectral_coeff(
            jnp.mod(inst_id - others, inst_count).astype(jnp.float32), float(inst_count)
        )
        spectral_operator = jnp.einsum(
            "c,kcyo->kyo", row_entry, every_instant, precision=lax.Precision.HIGHEST
        )
        psi = psi - TAU * (middle_point + DISSIP * spread + spectral_operator + source)
    return psi[:, None]


def solution(mesh):
    placed = (
        P(None, "inst", "space", None),
        P("inst", "space", None),
        P(None, "inst", "space", None),
        P("inst", "space", None),
        P(None, "space"),
        P(None, "space"),
        P("space"),
        P(),
        P(None, "space"),
        P("space"),
        P(),
    )
    return jax.shard_map(
        shards,
        mesh=mesh,
        in_specs=placed,
        out_specs=P(None, "inst", "space", None),
        check_vma=False,
    )
```

profile of v0, /device:TPU:2, one launch (start us, length us, event | category | flops | bytes accessed | tf_op | source)
XLA Modules:
  0.0 505.2 jit_solution(14409982304165432410)
XLA Ops:
  8.0 38.1 %while.10 = (s32[]{:T(128)}, f32[4,3,16384]{2,1,0:T(4,128)}, f32[2,16]{1,0:T(2,128)}, f32[1,16]{1,0:T(1,128)S(1)}, f32[]{:T(128)}, /*index=5*/f32[4,3,16384]{2,1,0:T(4,128)}, f32[3,16]{1,0:T(4,128)}, s32[]{:T(128)}) while((s32[]{:T(128)}, f32[4,3,16384]{2,1,0:T(4,128)}, f32[2,16]{1,0:T(2,128)}, f32[1,16]{1,0:T(1,128)S(1)}, f32[]{:T(128)}, ...), condition=%wide.region_6.8_spmd, body=%wide.region_3.7_spmd.sunk | while | flops 6766594 | bytes 5637533 | solution.py:52
  11.1 4.3 fusion.108
  20.6 4.3 fusion.108
  30.1 4.3 fusion.108
  39.6 4.3 fusion.108
  47.3 6.4 %collective-permute-start.1 = (f32[5,1,1024]{2,1,0:T(1,128)S(1)}, f32[5,1,1024]{2,1,0:T(1,128)S(1)}, u32[]{:S(2)}, u32[]{:S(2)}) collective-permute-start(f32[5,1,1024]{2,1,0:T(1,128)S(1)} %get-tuple-element.159), channel_id=1, source_target_pairs={{1,0},{2,1},{3,2},{4,3},{5,4},{6,5},{7,6},{8,7},{9,8},{10,9},{11,1... | collective-permute-start | bytes 61448 | tf_op jit(solution)/shard_map/ppermute | solution.py:26
  56.5 10.4 %gather_fusion = f32[1024,5,8]{2,1,0:T(8,128)} fusion(f32[5,8,1024]{1,0,2:T(8,128)} %copy.184, s32[1024]{0:T(1024)S(1)} %fusion.60), kind=kCustom, calls=%fused_computation.clone | custom fusion | bytes 331776 | tf_op jit(solution)/shard_map/jit(_take)/gather | solution.py:138
  66.9 2.7 copy.185
  69.6 10.4 %gather_fusion.1 = f32[1024,5,8]{2,1,0:T(8,128)} fusion(f32[5,8,1024]{1,0,2:T(8,128)} %copy.184, s32[1024]{0:T(1024)S(1)} %fusion.61), kind=kCustom, calls=%fused_computation.1.clone | custom fusion | bytes 331776 | tf_op jit(solution)/shard_map/jit(_take)/gather | solution.py:137
  82.5 10.4 %gather_fusion.2 = f32[1024,5,8]{2,1,0:T(8,128)} fusion(f32[5,8,1024]{1,0,2:T(8,128)} %copy.184, s32[1024]{0:T(1024)S(1)} %fusion.62), kind=kCustom, calls=%fused_computation.2.clone | custom fusion | bytes 331776 | tf_op jit(solution)/shard_map/jit(_take)/gather | solution.py:136
  92.9 2.6 copy.189
  95.6 10.4 %gather_fusion.3 = f32[1024,5,8]{2,1,0:T(8,128)} fusion(f32[5,8,1024]{1,0,2:T(8,128)} %copy.184, s32[1024]{0:T(1024)S(1)} %fusion.63), kind=kCustom, calls=%fused_computation.3.clone | custom fusion | bytes 331776 | tf_op jit(solution)/shard_map/jit(_take)/gather | solution.py:135
  109.2 169.2 %all-reduce.80.cloned.1.call-done = f32[3,65536]{1,0:T(4,128)} async-done(((f32[3,65536]{1,0:T(4,128)}), f32[3,65536]{1,0:T(4,128)}) %all-reduce.80.cloned.1.call-update) | async-done | bytes 786448 | tf_op jit(solution)/shard_map/psum | solution.py:114
  279.1 11.6 %scatter_custom_fusion = f32[8192]{0:T(1024)S(1)} fusion(s32[2048]{0:T(1024)} %param.24, f32[2048]{0:T(1024)S(1)} %multiply_reduce_fusion.4, f32[]{:T(128)} %constant.59.clone.1), kind=kCustom, calls=%fused_computation.205 | custom fusion | flops 2048 | bytes 33280 | tf_op jit(solution)/shard_map/scatter-add | solution.py:119
  290.8 3.2 fusion.9
  294.2 2.7 copy.192
  296.8 10.4 %gather_fusion.4 = f32[1024,5,8]{2,1,0:T(8,128)} fusion(f32[5,8,1024]{1,0,2:T(8,128)} %copy.192, s32[1024]{0:T(1024)S(1)} %fusion.60), kind=kCustom, calls=%fused_computation.4.clone | custom fusion | bytes 331776 | tf_op jit(solution)/shard_map/jit(_take)/gather | solution.py:138
  307.2 10.3 %gather_fusion.5 = f32[1024,5,8]{2,1,0:T(8,128)} fusion(f32[5,8,1024]{1,0,2:T(8,128)} %copy.192, s32[1024]{0:T(1024)S(1)} %fusion.61), kind=kCustom, calls=%fused_computation.5.clone | custom fusion | bytes 331776 | tf_op jit(solution)/shard_map/jit(_take)/gather | solution.py:137
  317.5 10.4 %gather_fusion.6 = f32[1024,5,8]{2,1,0:T(8,128)} fusion(f32[5,8,1024]{1,0,2:T(8,128)} %copy.192, s32[1024]{0:T(1024)S(1)} %fusion.62), kind=kCustom, calls=%fused_computation.6.clone | custom fusion | bytes 331776 | tf_op jit(solution)/shard_map/jit(_take)/gather | solution.py:136
  327.9 10.4 %gather_fusion.7 = f32[1024,5,8]{2,1,0:T(8,128)} fusion(f32[5,8,1024]{1,0,2:T(8,128)} %copy.192, s32[1024]{0:T(1024)S(1)} %fusion.63), kind=kCustom, calls=%fused_computation.7.clone | custom fusion | bytes 331776 | tf_op jit(solution)/shard_map/jit(_take)/gather | solution.py:135
  343.5 2.6 copy.197
  349.1 4.1 collective-permute-start.3
  355.0 37.8 %all-gather.8.cloned.1.call-done = f32[5,64,1024]{2,1,0:T(8,128)} async-done(((f32[5,8,1024]{2,1,0:T(8,128)}), f32[5,64,1024]{2,1,0:T(8,128)}) %all-gather.8.cloned.1.call-update) | async-done | bytes 1310736 | tf_op jit(solution)/shard_map/all_gather | solution.py:143
  392.8 3.2 fusion.7
  396.2 2.7 copy.200
  398.8 10.4 %gather_fusion.8 = f32[1024,5,8]{2,1,0:T(8,128)} fusion(f32[5,8,1024]{1,0,2:T(8,128)} %copy.200, s32[1024]{0:T(1024)S(1)} %fusion.60), kind=kCustom, calls=%fused_computation.8.clone | custom fusion | bytes 331776 | tf_op jit(solution)/shard_map/jit(_take)/gather | solution.py:138
  409.2 10.3 %gather_fusion.9 = f32[1024,5,8]{2,1,0:T(8,128)} fusion(f32[5,8,1024]{1,0,2:T(8,128)} %copy.200, s32[1024]{0:T(1024)S(1)} %fusion.61), kind=kCustom, calls=%fused_computation.9.clone | custom fusion | bytes 331776 | tf_op jit(solution)/shard_map/jit(_take)/gather | solution.py:137
  419.5 10.4 %gather_fusion.10 = f32[1024,5,8]{2,1,0:T(8,128)} fusion(f32[5,8,1024]{1,0,2:T(8,128)} %copy.200, s32[1024]{0:T(1024)S(1)} %fusion.62), kind=kCustom, calls=%fused_computation.10.clone | custom fusion | bytes 331776 | tf_op jit(solution)/shard_map/jit(_take)/gather | solution.py:136
  429.9 10.4 %gather_fusion.11 = f32[1024,5,8]{2,1,0:T(8,128)} fusion(f32[5,8,1024]{1,0,2:T(8,128)} %copy.200, s32[1024]{0:T(1024)S(1)} %fusion.63), kind=kCustom, calls=%fused_computation.11.clone | custom fusion | bytes 331776 | tf_op jit(solution)/shard_map/jit(_take)/gather | solution.py:135
  451.1 3.8 collective-permute-start.5
  456.8 36.8 %all-gather.10.cloned.1.call-done = f32[5,64,1024]{2,1,0:T(8,128)} async-done(((f32[5,8,1024]{2,1,0:T(8,128)}), f32[5,64,1024]{2,1,0:T(8,128)}) %all-gather.10.cloned.1.call-update) | async-done | bytes 1310736 | tf_op jit(solution)/shard_map/all_gather | solution.py:143
  493.6 3.2 fusion.5
  (121 shorter events, 55.6 us)
Async XLA Ops:
  7.4 270.9 %all-reduce.80.cloned.1.call-start = ((), (), s32[]{:S(2)}) async-start(), calls=%async_computation.1 | async-start | bytes 2097152 | tf_op jit(solution)/shard_map/psum | solution.py:114
  8.0 45.8 %copy-start.4 = (f32[5,1,8,1024]{3,2,1,0:T(8,128)S(1)}, f32[5,1,8,1024]{3,2,1,0:T(8,128)}, u32[]{:S(2)}) copy-start(f32[5,1,8,1024]{3,2,1,0:T(8,128)} %param.15) | copy-start | bytes 491524
  46.1 10.3 %copy-start.9 = (s32[4,1024]{1,0:T(4,128)S(1)}, s32[4,1024]{1,0:T(4,128)}, u32[]{:S(2)}) copy-start(s32[4,1024]{1,0:T(4,128)} %param.25) | copy-start | bytes 49156
  46.2 244.6 %all-gather.6.cloned.1.call-start = ((), (), s32[]{:S(2)}) async-start(), calls=%async_computation | async-start | bytes 1474560 | tf_op jit(solution)/shard_map/all_gather | solution.py:143
  47.3 61.6 %collective-permute-start = (f32[5,1,1024]{2,1,0:T(1,128)S(1)}, f32[5,1,1024]{2,1,0:T(1,128)S(1)}, u32[]{:S(2)}, u32[]{:S(2)}) collective-permute-start(f32[5,1,1024]{2,1,0:T(1,128)S(1)} %get-tuple-element.160), channel_id=1, source_target_pairs={{0,1},{1,2},{2,3},{3,4},{4,5},{5,6},{6,7},{7,8},{8,9},{9,10},{10,1... | collective-permute-start | bytes 61448 | tf_op jit(solution)/shard_map/ppermute | solution.py:24
  47.3 61.5 %collective-permute-start.1 = (f32[5,1,1024]{2,1,0:T(1,128)S(1)}, f32[5,1,1024]{2,1,0:T(1,128)S(1)}, u32[]{:S(2)}, u32[]{:S(2)}) collective-permute-start(f32[5,1,1024]{2,1,0:T(1,128)S(1)} %get-tuple-element.159), channel_id=1, source_target_pairs={{1,0},{2,1},{3,2},{4,3},{5,4},{6,5},{7,6},{8,7},{9,8},{10,9},{11,1... | collective-permute-start | bytes 61448 | tf_op jit(solution)/shard_map/ppermute | solution.py:26
  53.8 339.0 %all-gather.8.cloned.1.call-start = ((), (), s32[]{:S(2)}) async-start(), calls=%async_computation.2 | async-start | bytes 1474560 | tf_op jit(solution)/shard_map/all_gather | solution.py:143
  92.9 15.7 %copy-start.5 = (f32[1,8,1024]{2,1,0:T(8,128)S(1)}, f32[1,8,1024]{2,1,0:T(8,128)}, u32[]{:S(2)}) copy-start(f32[1,8,1024]{2,1,0:T(8,128)} %param.16) | copy-start | bytes 98308
  92.9 15.7 %copy-start.6 = (f32[3,1,8,1024]{3,2,1,0:T(8,128)S(1)}, f32[3,1,8,1024]{3,2,1,0:T(8,128)}, u32[]{:S(2)}) copy-start(f32[3,1,8,1024]{3,2,1,0:T(8,128)} %param.17) | copy-start | bytes 294916
  92.9 15.8 %copy-start.7 = (f32[1,8,1024]{2,1,0:T(8,128)S(1)}, f32[1,8,1024]{2,1,0:T(8,128)}, u32[]{:S(2)}) copy-start(f32[1,8,1024]{2,1,0:T(8,128)} %param.18) | copy-start | bytes 98308
  106.0 3.0 copy-start.10
  106.0 172.4 %copy-start.8 = (f32[3,2048]{1,0:T(4,128)S(1)}, f32[3,2048]{1,0:T(4,128)}, u32[]{:S(2)}) copy-start(f32[3,2048]{1,0:T(4,128)} %param.23) | copy-start | bytes 73732
  294.1 44.1 %copy-start.2 = (f32[5,8,1024]{2,1,0:T(8,128)}, f32[5,8,1024]{2,1,0:T(8,128)S(1)}, u32[]{:S(2)}) copy-start(f32[5,8,1024]{2,1,0:T(8,128)S(1)} %fusion.36) | copy-start | bytes 491524
  338.3 155.3 %all-gather.10.cloned.1.call-start = ((), (), s32[]{:S(2)}) async-start(), calls=%async_computation.3 | async-start | bytes 1474560 | tf_op jit(solution)/shard_map/all_gather | solution.py:143
  343.5 5.2 %copy-start.3 = (f32[5,8,1024]{2,1,0:T(8,128)S(1)}, f32[5,8,1024]{2,1,0:T(8,128)}, u32[]{:S(2)}) copy-start(f32[5,8,1024]{2,1,0:T(8,128)} %copy-done.2) | copy-start | bytes 491524
  348.8 5.8 %collective-permute-start.2 = (f32[5,1,1024]{2,1,0:T(1,128)S(1)}, f32[5,1,1024]{2,1,0:T(1,128)S(1)}, u32[]{:S(2)}, u32[]{:S(2)}) collective-permute-start(f32[5,1,1024]{2,1,0:T(1,128)S(1)} %get-tuple-element.148), channel_id=1, source_target_pairs={{0,1},{1,2},{2,3},{3,4},{4,5},{5,6},{6,7},{7,8},{8,9},{9,10},{10,1... | collective-permute-start | bytes 61448 | tf_op jit(solution)/shard_map/ppermute | solution.py:24
  349.1 5.6 %collective-permute-start.3 = (f32[5,1,1024]{2,1,0:T(1,128)S(1)}, f32[5,1,1024]{2,1,0:T(1,128)S(1)}, u32[]{:S(2)}, u32[]{:S(2)}) collective-permute-start(f32[5,1,1024]{2,1,0:T(1,128)S(1)} %get-tuple-element.147), channel_id=1, source_target_pairs={{1,0},{2,1},{3,2},{4,3},{5,4},{6,5},{7,6},{8,7},{9,8},{10,9},{11,1... | collective-permute-start | bytes 61448 | tf_op jit(solution)/shard_map/ppermute | solution.py:26
  396.2 44.1 %copy-start = (f32[5,8,1024]{2,1,0:T(8,128)}, f32[5,8,1024]{2,1,0:T(8,128)S(1)}, u32[]{:S(2)}) copy-start(f32[5,8,1024]{2,1,0:T(8,128)S(1)} %fusion.25) | copy-start | bytes 491524
  445.5 5.2 %copy-start.1 = (f32[5,8,1024]{2,1,0:T(8,128)S(1)}, f32[5,8,1024]{2,1,0:T(8,128)}, u32[]{:S(2)}) copy-start(f32[5,8,1024]{2,1,0:T(8,128)} %copy-done) | copy-start | bytes 491524
  450.8 5.7 %collective-permute-start.4 = (f32[5,1,1024]{2,1,0:T(1,128)S(1)}, f32[5,1,1024]{2,1,0:T(1,128)S(1)}, u32[]{:S(2)}, u32[]{:S(2)}) collective-permute-start(f32[5,1,1024]{2,1,0:T(1,128)S(1)} %get-tuple-element.137), channel_id=1, source_target_pairs={{0,1},{1,2},{2,3},{3,4},{4,5},{5,6},{6,7},{7,8},{8,9},{9,10},{10,1... | collective-permute-start | bytes 61448 | tf_op jit(solution)/shard_map/ppermute | solution.py:24
  451.1 5.4 %collective-permute-start.5 = (f32[5,1,1024]{2,1,0:T(1,128)S(1)}, f32[5,1,1024]{2,1,0:T(1,128)S(1)}, u32[]{:S(2)}, u32[]{:S(2)}) collective-permute-start(f32[5,1,1024]{2,1,0:T(1,128)S(1)} %get-tuple-element.136), channel_id=1, source_target_pairs={{1,0},{2,1},{3,2},{4,3},{5,4},{6,5},{7,6},{8,7},{9,8},{10,9},{11,1... | collective-permute-start | bytes 61448 | tf_op jit(solution)/shard_map/ppermute | solution.py:26
Sparse Core Ops, SparseCore 0:
  46.3 231.9 all-reduce.79
Sparse Core Ops, SparseCore 1:
  53.8 54.9 all-gather.5
  338.4 54.4 all-gather.7
  440.4 53.2 all-gather.9
where the time goes:
time: 506 us; the launch traced here: 505 us
  waiting for transfers between devices  247 us (49%)
  local copies, waits for them, and re-layouts  175 us (35%)
  other arithmetic  43.5 us (9%)
  between operations  15.5 us (3%)
  starting transfers between devices  15.1 us (3%)
  matrix products  9.46 us (2%)
    psum x1, waiting for transfers between devices, shards(): total = lax.psum(whole, 'space')  169 us
    all_gather x3, waiting for transfers between devices, shards(): every_instant = lax.all_gather(psi[:, None], 'inst', axis=1, tiled=True)  74.7 us
    gather x6, local copies, waits for them, and re-layouts, shards(): minus_y = jnp.take(psi, plane_nbr[1], axis=2)  39.1 us
    gather x6, local copies, waits for them, and re-layouts, shards(): plus_y = jnp.take(psi, plane_nbr[0], axis=2)  39 us
    gather x6, local copies, waits for them, and re-layouts, shards(): minus_z = jnp.take(psi, plane_nbr[3], axis=2)  38.9 us
    gather x6, local copies, waits for them, and re-layouts, shards(): plus_z = jnp.take(psi, plane_nbr[2], axis=2)  38.8 us
    div x4, other arithmetic, panel_block(): (observers[3][:, None] * jnp.cos(phase) + observers[4][:, None] * jnp.sin...  17.3 us
    ppermute x3, starting transfers between devices, padded_2(): lax.ppermute(head, axis, [((i + 1) % count, i) for i in range(count)])  14.3 us
  transfers between devices with their start and end apart: 10, of which 5 were waited for; matrix products, arithmetic and copies ran while one was open for 18% of the time, Pallas kernels for 0%

commit v1 on v0

--- a/solution.py
+++ b/solution.py
@@ -140,7 +140,9 @@
             (0.5 * (minus_a - plus_a), 0.5 * (minus_y - plus_y), 0.5 * (minus_z - plus_z))
         )[0]
         spread = 6.0 * psi - (minus_a + plus_a + plus_y + minus_y + plus_z + minus_z)
-        every_instant = lax.all_gather(psi[:, None], "inst", axis=1, tiled=True)
+        every_instant = jnp.concatenate(
+            lax.all_to_all(jnp.stack([psi[:, None]] * lax.axis_size("inst")), "inst", 0, 0), axis=1
+        )
         others = jnp.arange(inst_count, dtype=jnp.int32)
         row_entry = spectral_coeff(
             jnp.mod(inst_id - others, inst_count).astype(jnp.float32), float(inst_count)

time: 506 us -> 477 us (0.943)
  waiting for transfers between devices: 247 us -> 200 us
  starting transfers between devices: 15.1 us -> 33.7 us
    all_gather x3 -> x0, waiting for transfers between devices: 74.7 us -> none  [shards(): every_instant = lax.all_gather(psi[:, None], 'inst', axis=1, tiled=True)]
    all_to_all x0 -> x3, waiting for transfers between devices: none -> 30.9 us  [shards(): lax.all_to_all(jnp.stack([psi[:, None]] * lax.axis_size('inst')), 'inst',...]
    all_to_all x0 -> x3, starting transfers between devices: none -> 18.8 us  [shards(): lax.all_to_all(jnp.stack([psi[:, None]] * lax.axis_size('inst')), 'inst',...]
  transfers between devices with their start and end apart: 10 -> 10, of which waited for: 5 -> 3; matrix products, arithmetic and copies ran while one was open for 18% -> 23% of each run, Pallas kernels for 0% -> 0%
where the time goes in v1:
time: 477 us; the launch traced here: 474 us
  waiting for transfers between devices  200 us (42%)
  local copies, waits for them, and re-layouts  178 us (37%)
  other arithmetic  43.5 us (9%)
  starting transfers between devices  33.7 us (7%)
  between operations  13.8 us (3%)
  matrix products  5.52 us (1%)
    psum x1, waiting for transfers between devices, shards(): total = lax.psum(whole, 'space')  169 us
    gather x6, local copies, waits for them, and re-layouts, shards(): plus_y = jnp.take(psi, plane_nbr[0], axis=2)  38.9 us
    gather x6, local copies, waits for them, and re-layouts, shards(): minus_z = jnp.take(psi, plane_nbr[3], axis=2)  38.9 us
    gather x6, local copies, waits for them, and re-layouts, shards(): plus_z = jnp.take(psi, plane_nbr[2], axis=2)  38.8 us
    gather x6, local copies, waits for them, and re-layouts, shards(): minus_y = jnp.take(psi, plane_nbr[1], axis=2)  38.8 us
    all_to_all x3, waiting for transfers between devices, shards(): lax.all_to_all(jnp.stack([psi[:, None]] * lax.axis_size('inst')), 'inst',...  30.9 us
    all_to_all x3, starting transfers between devices, shards(): lax.all_to_all(jnp.stack([psi[:, None]] * lax.axis_size('inst')), 'inst',...  18.8 us
    div x4, other arithmetic, panel_block(): (observers[3][:, None] * jnp.cos(phase) + observers[4][:, None] * jnp.sin...  17.3 us
  transfers between devices with their start and end apart: 10, of which 3 were waited for; matrix products, arithmetic and copies ran while one was open for 23% of the time, Pallas kernels for 0%

profile of v1, /device:TPU:2, one launch (start us, length us, event | category | flops | bytes accessed | tf_op | source)
XLA Modules:
  0.0 474.4 jit_solution(9735607217026168248)
XLA Ops:
  7.7 6.4 %collective-permute-start.1 = (f32[5,1,1024]{2,1,0:T(1,128)S(1)}, f32[5,1,1024]{2,1,0:T(1,128)S(1)}, u32[]{:S(2)}, u32[]{:S(2)}) collective-permute-start(f32[5,1,1024]{2,1,0:T(1,128)S(1)} %get-tuple-element.159), channel_id=1, source_target_pairs={{1,0},{2,1},{3,2},{4,3},{5,4},{6,5},{7,6},{8,7},{9,8},{10,9},{11,1... | collective-permute-start | bytes 61448 | tf_op jit(solution)/shard_map/ppermute | solution.py:26
  14.7 38.1 %while.10 = (s32[]{:T(128)}, f32[4,3,16384]{2,1,0:T(4,128)}, f32[2,16]{1,0:T(2,128)}, f32[1,16]{1,0:T(1,128)S(1)}, f32[]{:T(128)}, /*index=5*/f32[4,3,16384]{2,1,0:T(4,128)}, f32[3,16]{1,0:T(4,128)}, s32[]{:T(128)}) while((s32[]{:T(128)}, f32[4,3,16384]{2,1,0:T(4,128)}, f32[2,16]{1,0:T(2,128)}, f32[1,16]{1,0:T(1,128)S(1)}, f32[]{:T(128)}, ...), condition=%wide.region_6.8_spmd, body=%wide.region_3.7_spmd.sunk | while | flops 6766594 | bytes 5637533 | solution.py:52
  17.7 4.3 fusion.108
  27.2 4.3 fusion.108
  36.8 4.3 fusion.108
  46.3 4.3 fusion.108
  54.1 7.2 %all-to-all-start = ((f32[8,5,1,8,1024]{4,3,2,1,0:T(8,128)}), f32[8,5,1,8,1024]{4,3,2,1,0:T(8,128)S(1)}, u32[]{:S(2)}, u32[]{:S(2)}) async-start(f32[8,5,1,8,1024]{4,3,2,1,0:T(8,128)} %stack.9), calls=%async_computation | async-start | bytes 2621440 | tf_op jit(solution)/shard_map/all_to_all | solution.py:144
  64.0 10.3 %gather_fusion = f32[1024,5,8]{2,1,0:T(8,128)} fusion(f32[5,8,1024]{1,0,2:T(8,128)} %copy.190, s32[1024]{0:T(1024)S(1)} %fusion.60), kind=kCustom, calls=%fused_computation.clone | custom fusion | bytes 331776 | tf_op jit(solution)/shard_map/jit(_take)/gather | solution.py:138
  74.4 2.6 copy.191
  77.0 10.4 %gather_fusion.1 = f32[1024,5,8]{2,1,0:T(8,128)} fusion(f32[5,8,1024]{1,0,2:T(8,128)} %copy.190, s32[1024]{0:T(1024)S(1)} %fusion.61), kind=kCustom, calls=%fused_computation.1.clone | custom fusion | bytes 331776 | tf_op jit(solution)/shard_map/jit(_take)/gather | solution.py:137
  90.0 10.3 %gather_fusion.2 = f32[1024,5,8]{2,1,0:T(8,128)} fusion(f32[5,8,1024]{1,0,2:T(8,128)} %copy.190, s32[1024]{0:T(1024)S(1)} %fusion.62), kind=kCustom, calls=%fused_computation.2.clone | custom fusion | bytes 331776 | tf_op jit(solution)/shard_map/jit(_take)/gather | solution.py:136
  100.3 2.6 copy.195
  103.0 10.4 %gather_fusion.3 = f32[1024,5,8]{2,1,0:T(8,128)} fusion(f32[5,8,1024]{1,0,2:T(8,128)} %copy.190, s32[1024]{0:T(1024)S(1)} %fusion.63), kind=kCustom, calls=%fused_computation.3.clone | custom fusion | bytes 331776 | tf_op jit(solution)/shard_map/jit(_take)/gather | solution.py:135
  113.3 2.6 copy.197
  116.4 168.7 %all-reduce.80.cloned.1.call-done = f32[3,65536]{1,0:T(4,128)} async-done(((f32[3,65536]{1,0:T(4,128)}), f32[3,65536]{1,0:T(4,128)}) %all-reduce.80.cloned.1.call-update) | async-done | bytes 786448 | tf_op jit(solution)/shard_map/psum | solution.py:114
  285.9 11.6 %scatter_custom_fusion = f32[8192]{0:T(1024)S(1)} fusion(s32[2048]{0:T(1024)} %param.24, f32[2048]{0:T(1024)S(1)} %multiply_reduce_fusion.4, f32[]{:T(128)} %constant.59.clone.1), kind=kCustom, calls=%fused_computation.205 | custom fusion | flops 2048 | bytes 33280 | tf_op jit(solution)/shard_map/scatter-add | solution.py:119
  299.6 2.6 copy.198
  302.2 10.4 %gather_fusion.4 = f32[1024,5,8]{2,1,0:T(8,128)} fusion(f32[5,8,1024]{1,0,2:T(8,128)} %copy.198, s32[1024]{0:T(1024)S(1)} %fusion.60), kind=kCustom, calls=%fused_computation.4.clone | custom fusion | bytes 331776 | tf_op jit(solution)/shard_map/jit(_take)/gather | solution.py:138
  312.6 10.3 %gather_fusion.5 = f32[1024,5,8]{2,1,0:T(8,128)} fusion(f32[5,8,1024]{1,0,2:T(8,128)} %copy.198, s32[1024]{0:T(1024)S(1)} %fusion.61), kind=kCustom, calls=%fused_computation.5.clone | custom fusion | bytes 331776 | tf_op jit(solution)/shard_map/jit(_take)/gather | solution.py:137
  322.9 10.3 %gather_fusion.6 = f32[1024,5,8]{2,1,0:T(8,128)} fusion(f32[5,8,1024]{1,0,2:T(8,128)} %copy.198, s32[1024]{0:T(1024)S(1)} %fusion.62), kind=kCustom, calls=%fused_computation.6.clone | custom fusion | bytes 331776 | tf_op jit(solution)/shard_map/jit(_take)/gather | solution.py:136
  333.2 10.4 %gather_fusion.7 = f32[1024,5,8]{2,1,0:T(8,128)} fusion(f32[5,8,1024]{1,0,2:T(8,128)} %copy.198, s32[1024]{0:T(1024)S(1)} %fusion.63), kind=kCustom, calls=%fused_computation.7.clone | custom fusion | bytes 331776 | tf_op jit(solution)/shard_map/jit(_take)/gather | solution.py:135
  354.3 4.1 collective-permute-start.3
  359.6 7.0 %all-to-all-start.1 = ((f32[8,5,1,8,1024]{4,3,2,1,0:T(8,128)}), f32[8,5,1,8,1024]{4,3,2,1,0:T(8,128)S(1)}, u32[]{:S(2)}, u32[]{:S(2)}) async-start(f32[8,5,1,8,1024]{4,3,2,1,0:T(8,128)} %stack.10), calls=%async_computation.1 | async-start | bytes 2621440 | tf_op jit(solution)/shard_map/all_to_all | solution.py:144
  367.0 15.2 %all-to-all-done.1 = f32[8,5,1,8,1024]{4,3,2,1,0:T(8,128)S(1)} async-done(((f32[8,5,1,8,1024]{4,3,2,1,0:T(8,128)}), f32[8,5,1,8,1024]{4,3,2,1,0:T(8,128)S(1)}, u32[]{:S(2)}, u32[]{:S(2)}) %all-to-all-start.1) | async-done | bytes 1310752 | tf_op jit(solution)/shard_map/all_to_all | solution.py:144
  384.2 2.6 copy.206
  386.8 10.4 %gather_fusion.8 = f32[1024,5,8]{2,1,0:T(8,128)} fusion(f32[5,8,1024]{1,0,2:T(8,128)} %copy.206, s32[1024]{0:T(1024)S(1)} %fusion.60), kind=kCustom, calls=%fused_computation.8.clone | custom fusion | bytes 331776 | tf_op jit(solution)/shard_map/jit(_take)/gather | solution.py:138
  397.2 10.3 %gather_fusion.9 = f32[1024,5,8]{2,1,0:T(8,128)} fusion(f32[5,8,1024]{1,0,2:T(8,128)} %copy.206, s32[1024]{0:T(1024)S(1)} %fusion.61), kind=kCustom, calls=%fused_computation.9.clone | custom fusion | bytes 331776 | tf_op jit(solution)/shard_map/jit(_take)/gather | solution.py:137
  407.5 10.3 %gather_fusion.10 = f32[1024,5,8]{2,1,0:T(8,128)} fusion(f32[5,8,1024]{1,0,2:T(8,128)} %copy.206, s32[1024]{0:T(1024)S(1)} %fusion.62), kind=kCustom, calls=%fused_computation.10.clone | custom fusion | bytes 331776 | tf_op jit(solution)/shard_map/jit(_take)/gather | solution.py:136
  417.8 10.4 %gather_fusion.11 = f32[1024,5,8]{2,1,0:T(8,128)} fusion(f32[5,8,1024]{1,0,2:T(8,128)} %copy.206, s32[1024]{0:T(1024)S(1)} %fusion.63), kind=kCustom, calls=%fused_computation.11.clone | custom fusion | bytes 331776 | tf_op jit(solution)/shard_map/jit(_take)/gather | solution.py:135
  439.0 3.8 collective-permute-start.5
  444.1 4.6 all-to-all-start.2
  449.1 15.7 %all-to-all-done.2 = f32[8,5,1,8,1024]{4,3,2,1,0:T(8,128)S(1)} async-done(((f32[8,5,1,8,1024]{4,3,2,1,0:T(8,128)}), f32[8,5,1,8,1024]{4,3,2,1,0:T(8,128)S(1)}, u32[]{:S(2)}, u32[]{:S(2)}) %all-to-all-start.2) | async-done | bytes 1310752 | tf_op jit(solution)/shard_map/all_to_all | solution.py:144
  (113 shorter events, 61.7 us)
Async XLA Ops:
  6.5 278.6 %all-reduce.80.cloned.1.call-start = ((), (), s32[]{:S(2)}) async-start(), calls=%async_computation.3 | async-start | bytes 2097152 | tf_op jit(solution)/shard_map/psum | solution.py:114
  7.6 108.5 %collective-permute-start = (f32[5,1,1024]{2,1,0:T(1,128)S(1)}, f32[5,1,1024]{2,1,0:T(1,128)S(1)}, u32[]{:S(2)}, u32[]{:S(2)}) collective-permute-start(f32[5,1,1024]{2,1,0:T(1,128)S(1)} %get-tuple-element.160), channel_id=1, source_target_pairs={{0,1},{1,2},{2,3},{3,4},{4,5},{5,6},{6,7},{7,8},{8,9},{9,10},{10,1... | collective-permute-start | bytes 61448 | tf_op jit(solution)/shard_map/ppermute | solution.py:24
  7.7 108.4 %collective-permute-start.1 = (f32[5,1,1024]{2,1,0:T(1,128)S(1)}, f32[5,1,1024]{2,1,0:T(1,128)S(1)}, u32[]{:S(2)}, u32[]{:S(2)}) collective-permute-start(f32[5,1,1024]{2,1,0:T(1,128)S(1)} %get-tuple-element.159), channel_id=1, source_target_pairs={{1,0},{2,1},{3,2},{4,3},{5,4},{6,5},{7,6},{8,7},{9,8},{10,9},{11,1... | collective-permute-start | bytes 61448 | tf_op jit(solution)/shard_map/ppermute | solution.py:26
  14.7 38.1 %copy-start = (f32[5,1,8,1024]{3,2,1,0:T(8,128)S(1)}, f32[5,1,8,1024]{3,2,1,0:T(8,128)}, u32[]{:S(2)}) copy-start(f32[5,1,8,1024]{3,2,1,0:T(8,128)} %param.15) | copy-start | bytes 491524
  52.8 11.1 %copy-start.5 = (s32[4,1024]{1,0:T(4,128)S(1)}, s32[4,1024]{1,0:T(4,128)}, u32[]{:S(2)}) copy-start(s32[4,1024]{1,0:T(4,128)} %param.25) | copy-start | bytes 49156
  54.1 243.4 %all-to-all-start = ((f32[8,5,1,8,1024]{4,3,2,1,0:T(8,128)}), f32[8,5,1,8,1024]{4,3,2,1,0:T(8,128)S(1)}, u32[]{:S(2)}, u32[]{:S(2)}) async-start(f32[8,5,1,8,1024]{4,3,2,1,0:T(8,128)} %stack.9), calls=%async_computation | async-start | bytes 2621440 | tf_op jit(solution)/shard_map/all_to_all | solution.py:144
  74.3 15.6 %copy-start.1 = (f32[1,8,1024]{2,1,0:T(8,128)S(1)}, f32[1,8,1024]{2,1,0:T(8,128)}, u32[]{:S(2)}) copy-start(f32[1,8,1024]{2,1,0:T(8,128)} %param.16) | copy-start | bytes 98308
  74.4 15.6 %copy-start.2 = (f32[3,1,8,1024]{3,2,1,0:T(8,128)S(1)}, f32[3,1,8,1024]{3,2,1,0:T(8,128)}, u32[]{:S(2)}) copy-start(f32[3,1,8,1024]{3,2,1,0:T(8,128)} %param.17) | copy-start | bytes 294916
  100.3 15.6 %copy-start.3 = (f32[1,8,1024]{2,1,0:T(8,128)S(1)}, f32[1,8,1024]{2,1,0:T(8,128)}, u32[]{:S(2)}) copy-start(f32[1,8,1024]{2,1,0:T(8,128)} %param.18) | copy-start | bytes 98308
  103.0 13.3 %copy-start.6 = (pred[3]{0:T(512)(128)(4,1)S(1)}, pred[3]{0:T(512)(128)(4,1)}, u32[]{:S(2)}) copy-start(pred[3]{0:T(512)(128)(4,1)} %constant.63.clone.1) | copy-start | bytes 13
  113.3 171.8 %copy-start.4 = (f32[3,2048]{1,0:T(4,128)S(1)}, f32[3,2048]{1,0:T(4,128)}, u32[]{:S(2)}) copy-start(f32[3,2048]{1,0:T(4,128)} %param.23) | copy-start | bytes 73732
  354.1 12.6 %collective-permute-start.2 = (f32[5,1,1024]{2,1,0:T(1,128)S(1)}, f32[5,1,1024]{2,1,0:T(1,128)S(1)}, u32[]{:S(2)}, u32[]{:S(2)}) collective-permute-start(f32[5,1,1024]{2,1,0:T(1,128)S(1)} %get-tuple-element.148), channel_id=1, source_target_pairs={{0,1},{1,2},{2,3},{3,4},{4,5},{5,6},{6,7},{7,8},{8,9},{9,10},{10,1... | collective-permute-start | bytes 61448 | tf_op jit(solution)/shard_map/ppermute | solution.py:24
  354.3 12.3 %collective-permute-start.3 = (f32[5,1,1024]{2,1,0:T(1,128)S(1)}, f32[5,1,1024]{2,1,0:T(1,128)S(1)}, u32[]{:S(2)}, u32[]{:S(2)}) collective-permute-start(f32[5,1,1024]{2,1,0:T(1,128)S(1)} %get-tuple-element.147), channel_id=1, source_target_pairs={{1,0},{2,1},{3,2},{4,3},{5,4},{6,5},{7,6},{8,7},{9,8},{10,9},{11,1... | collective-permute-start | bytes 61448 | tf_op jit(solution)/shard_map/ppermute | solution.py:26
  359.6 22.5 %all-to-all-start.1 = ((f32[8,5,1,8,1024]{4,3,2,1,0:T(8,128)}), f32[8,5,1,8,1024]{4,3,2,1,0:T(8,128)S(1)}, u32[]{:S(2)}, u32[]{:S(2)}) async-start(f32[8,5,1,8,1024]{4,3,2,1,0:T(8,128)} %stack.10), calls=%async_computation.1 | async-start | bytes 2621440 | tf_op jit(solution)/shard_map/all_to_all | solution.py:144
  438.7 10.1 %collective-permute-start.4 = (f32[5,1,1024]{2,1,0:T(1,128)S(1)}, f32[5,1,1024]{2,1,0:T(1,128)S(1)}, u32[]{:S(2)}, u32[]{:S(2)}) collective-permute-start(f32[5,1,1024]{2,1,0:T(1,128)S(1)} %get-tuple-element.137), channel_id=1, source_target_pairs={{0,1},{1,2},{2,3},{3,4},{4,5},{5,6},{6,7},{7,8},{8,9},{9,10},{10,1... | collective-permute-start | bytes 61448 | tf_op jit(solution)/shard_map/ppermute | solution.py:24
  439.0 9.8 %collective-permute-start.5 = (f32[5,1,1024]{2,1,0:T(1,128)S(1)}, f32[5,1,1024]{2,1,0:T(1,128)S(1)}, u32[]{:S(2)}, u32[]{:S(2)}) collective-permute-start(f32[5,1,1024]{2,1,0:T(1,128)S(1)} %get-tuple-element.136), channel_id=1, source_target_pairs={{1,0},{2,1},{3,2},{4,3},{5,4},{6,5},{7,6},{8,7},{9,8},{10,9},{11,1... | collective-permute-start | bytes 61448 | tf_op jit(solution)/shard_map/ppermute | solution.py:26
  444.1 20.7 %all-to-all-start.2 = ((f32[8,5,1,8,1024]{4,3,2,1,0:T(8,128)}), f32[8,5,1,8,1024]{4,3,2,1,0:T(8,128)S(1)}, u32[]{:S(2)}, u32[]{:S(2)}) async-start(f32[8,5,1,8,1024]{4,3,2,1,0:T(8,128)} %stack.11), calls=%async_computation.2 | async-start | bytes 2621440 | tf_op jit(solution)/shard_map/all_to_all | solution.py:144
Sparse Core Ops, SparseCore 0:
  52.9 232.1 all-reduce.79
